TPU v7x, 32 devices: a whole 2x2x4 slice. The times are simulated.
32 devices in a mesh: groups: 2 (over x), section: 1, expert: 16 (over z, y, core).
Axes of the slice: x: 2, y: 2, z: 4, core: 2. Of those that a mesh axis runs over, the one named last changes fastest.
Arguments:
- inputs: bfloat16 [2, 512, 2048], P(None, ('groups', 'expert')), parts along dimension 1, may hold values from -6 to 6
- routes: int32 [2, 2, 512, 8], P('section', None, ('groups', 'expert')), parts along dimension 2, may hold values from 0 to 15, all different within a row; in each aligned block of 16 rows (0 to 15, 16 to 31, ..., all dimensions but the last counted through in order) at most 16 rows name the same one
- norm_gain: float32 [2, 2048], P('section'), may hold values from 0.1 to 1.9
- w_gate_up: bfloat16 [2, 16, 2048, 1536], P('section', 'expert'), may hold values from -0.125 to 0.125
- w_down: bfloat16 [2, 16, 768, 2048], P('section', 'expert'), may hold values from -0.4375 to 0.4375
Outputs:
- outputs: bfloat16 [2, 2, 512, 2048], P('section', None, ('groups', 'expert')), parts along dimension 2
There are 2 independent parts, one for each index of `groups`. A program takes and returns all parts, laid end to end along the dimension named above; an argument that names none is the same for every part. Nothing has to cross between parts.
Inputs may be any that keep to these rules, and one draw needn't show every extreme that they name: `routes`: the 8 entries of a row differ. In each aligned block of 16 rows (the rows of one index of expert in one micro-batch of one layer) no expert is named by more than 16 rows, and some block reaches 16.
All inputs are finite; a program needn't handle non-finite values.
Results may differ from a plain program's by a relative error of at most 0.0055.
Values may be sent and summed in bfloat16 or wider, within the bound.
A program may use at most 64 MiB of HBM per device.

v0:
```python
import functools

import jax
import jax.numpy as jnp
from jax import lax
from jax.experimental import pallas as pl
from jax.experimental.pallas import tpu as pltpu
from jax.sharding import PartitionSpec as P

eps = 1e-06


def from_behind(value, axis, steps):
    count = lax.axis_size(axis)
    initial, last = (max(0, -steps), min(count, count - steps))
    return lax.ppermute(value, axis, [(source, source + steps) for source in range(initial, last)])


def expert_rows(rows, gate_up, down_proj):
    hidden_size = down_proj.shape[0]
    joined = jnp.dot(rows, gate_up, preferred_element_type=jnp.float32)
    hidden = (jax.nn.silu(joined[:, :hidden_size]) * joined[:, hidden_size:]).astype(jnp.bfloat16)
    return jnp.dot(hidden, down_proj, preferred_element_type=jnp.float32).astype(jnp.bfloat16)


def run_experts(received, gate_up, down_proj):
    flat = received.reshape(-1, received.shape[2])
    done = expert_rows(flat, gate_up, down_proj)
    return done.reshape(received.shape)


def moe_layer(current, layer_routes, gain_row, gate_up, down_proj, experts, capacity):
    tokens, features = current.shape
    widened = current.astype(jnp.float32)
    scale_inv = lax.rsqrt(jnp.mean(widened * widened, axis=-1, keepdims=True) + eps)
    normed = (widened * scale_inv * gain_row).astype(jnp.bfloat16)
    expert_ids = jnp.arange(experts, dtype=jnp.int32)
    onehot = (layer_routes[:, :, None] == expert_ids[None, None, :]).astype(jnp.int32)
    counted = jnp.sum(onehot, axis=1)
    before = jnp.cumsum(counted, axis=0) - counted
    slot_of = jnp.sum(onehot * (expert_ids[None, None, :] * capacity + before[:, None, :]), axis=2)
    slot_ids = jnp.arange(experts * capacity, dtype=jnp.int32)
    placing = jnp.sum(
        (slot_ids[:, None, None] == slot_of[None, :, :]).astype(jnp.int32), axis=2
    ).astype(jnp.bfloat16)
    outgoing = jnp.dot(placing, normed, preferred_element_type=jnp.float32).astype(jnp.bfloat16)
    outgoing = outgoing.reshape(experts, capacity, features)
    results = run_experts(
        lax.all_to_all(outgoing, "expert", split_axis=0, concat_axis=0, tiled=True),
        gate_up,
        down_proj,
    )
    returned = lax.all_to_all(results, "expert", split_axis=0, concat_axis=0, tiled=True).reshape(
        experts * capacity, features
    )
    combined = (
        jnp.einsum("it,id->td", placing, returned, preferred_element_type=jnp.float32) * 0.125
    )
    return (widened + combined).astype(jnp.bfloat16)


def on_device(inputs, routes, norm_gain, w_gate_up, w_down):
    experts = lax.axis_size("expert")
    sections = lax.axis_size("section")
    batches, tokens, features = inputs.shape
    top_k = routes.shape[3]
    capacity = min(tokens, 2 * tokens * top_k // experts)
    if sections == 1:
        layers_out = []
        previous = [inputs[batch_no] for batch_no in range(batches)]
        for layer_no in range(routes.shape[0]):
            current_layer = []
            for batch_no in range(batches):
                current_layer.append(
                    moe_layer(
                        previous[batch_no],
                        routes[layer_no, batch_no],
                        norm_gain[layer_no],
                        w_gate_up[layer_no, 0],
                        w_down[layer_no, 0],
                        experts,
                        capacity,
                    )
                )
            layers_out.append(jnp.stack(current_layer))
            previous = current_layer
        return jnp.stack(layers_out)
    segment_no = lax.axis_index("section")
    layer_routes = routes[0]
    gain_row = norm_gain[0]
    gate_up = w_gate_up[0, 0]
    down_proj = w_down[0, 0]
    handed = jnp.zeros((tokens, features), jnp.bfloat16)
    finished = []
    for turn_no in range(batches + 1):
        if turn_no < batches:
            fresh_rows = inputs[turn_no]
        else:
            fresh_rows = jnp.zeros((tokens, features), jnp.bfloat16)
        current = jnp.where(segment_no == 0, fresh_rows, handed)
        batch_pick = jnp.clip(turn_no - segment_no, 0, batches - 1)
        turn_routes = lax.dynamic_index_in_dim(layer_routes, batch_pick, 0, keepdims=False)
        result = moe_layer(current, turn_routes, gain_row, gate_up, down_proj, experts, capacity)
        finished.append(result)
        if turn_no < batches:
            handed = from_behind(result, "section", 1)
    first_segment = jnp.stack(finished[:batches])
    second_segment = jnp.stack(finished[1:])
    return jnp.where(segment_no == 0, first_segment, second_segment)[None]

LANES = 128
PAIR = 2
TILE = 256


def flat_rows(block):
    return block.reshape(-1, block.shape[-1])


def moe_kernel(
    count,
    x_ref,
    routes_ref,
    gain_ref,
    gu_hbm,
    down_hbm,
    out_ref,
    gu,
    down,
    rows,
    hidden,
    made,
    from_core,
    to_y,
    from_y,
    to_z,
    from_z,
    w_sem,
    az_s,
    az_r,
    ay_s,
    ay_r,
    ac_s,
    ac_r,
    rc_s,
    rc_r,
    ry_s,
    ry_r,
    rz_s,
    rz_r,
):
    layers, batches = routes_ref.shape[0], routes_ref.shape[1]
    tokens, features = x_ref.shape[1], x_ref.shape[2]
    units = down.shape[1]
    depth = count // (PAIR * PAIR)
    me = lax.axis_index("expert")
    c = lax.rem(me, PAIR)
    y = lax.rem(lax.div(me, PAIR), PAIR)
    z = lax.div(me, PAIR * PAIR)
    other_c, other_y = 1 - c, 1 - y

    def expert_at(zz, yy, cc):
        return (zz * PAIR + yy) * PAIR + cc

    def z_up(k):
        return lax.rem(z + k, depth)

    core_peer = expert_at(z, y, other_c)
    y_peer = expert_at(z, other_y, c)

    def remote(src, dst, send, recv, target):
        return pltpu.make_async_remote_copy(
            src_ref=src,
            dst_ref=dst,
            send_sem=send,
            recv_sem=recv,
            device_id={"expert": target},
            device_id_type=pl.DeviceIdType.MESH,
        )

    loads = []
    for layer in range(layers):
        for number, (source, target) in enumerate(((gu_hbm, gu), (down_hbm, down))):
            load = pltpu.make_async_copy(
                source.at[layer, 0], target.at[layer], w_sem.at[layer, number]
            )
            load.start()
            loads.append(load)

    barrier = pltpu.get_barrier_semaphore()
    for peer in [expert_at(z_up(k), y, c) for k in range(1, depth)] + [core_peer, y_peer]:
        pl.semaphore_signal(
            barrier, inc=1, device_id={"expert": peer}, device_id_type=pl.DeviceIdType.MESH
        )
    pl.semaphore_wait(barrier, depth + 1)

    sends = []

    def go(copy):
        copy.start()
        sends.append(copy)

    def slot(layer, batch):
        return layer * batches + batch

    def nearest(n):
        chosen = z * 0
        for at in range(depth):
            ranked = sorted(range(depth), key=lambda v: (abs(v - at), v))
            chosen = jnp.where(z == at, ranked[n], chosen)
        return chosen

    near = [z] + [nearest(n) for n in range(1, depth)]

    def row_block(s, cc, yy, zz):
        if s == 0:
            return rows.at[s, cc, yy, zz]
        return rows.at[s, cc, yy, zz, :, pl.ds(0, features)]

    def gather_core(s, cc, yy, zz):
        block = row_block(s, cc, yy, zz)
        return remote(block, block, ac_s.at[s, yy, zz], ac_r.at[s, yy, zz], core_peer)

    def gather_y(s, yy, zz):
        block = row_block(s, c, yy, zz)
        return remote(block, block, ay_s.at[s, zz], ay_r.at[s, zz], y_peer)

    def norm_send(layer, batch):
        s = slot(layer, batch)
        h = (x_ref[batch] if layer == 0 else out_ref[layer - 1, batch]).astype(jnp.float32)
        scale = lax.rsqrt(jnp.mean(h * h, axis=-1, keepdims=True) + eps)
        normed = (h * scale * gain_ref[pl.ds(layer, 1), :]).astype(jnp.bfloat16)
        rows[s, c, y, z, :, pl.ds(0, features)] = normed
        if s == 0:
            lanes = lax.broadcasted_iota(jnp.int32, (tokens, LANES), 1)
            named = jnp.zeros((tokens, LANES), jnp.float32)
            for lay in range(layers):
                for bat in range(batches):
                    chosen = routes_ref[lay, bat] + slot(lay, bat) * count
                    for k in range(chosen.shape[1]):
                        named = named + (chosen[:, k : k + 1] == lanes).astype(jnp.float32)
            rows[s, c, y, z, :, pl.ds(features, LANES)] = named.astype(jnp.bfloat16)
        block = row_block(s, c, y, z)
        for n in range(1, depth):
            go(remote(block, block, az_s.at[s, near[n]], az_r.at[s, z], expert_at(near[n], y, c)))
        go(gather_y(s, y, z))
        go(gather_core(s, c, y, z))

    def gather_z_step(layer, batch, n):
        s = slot(layer, batch)
        zz = near[n]
        block = row_block(s, c, y, zz)
        remote(block, block, az_s.at[s, zz], az_r.at[s, zz], y_peer).wait_recv()
        go(gather_y(s, y, zz))
        go(gather_core(s, c, y, zz))

    def gather_y_step(layer, batch, n):
        s = slot(layer, batch)
        gather_y(s, other_y, near[n]).wait_recv()
        go(gather_core(s, c, other_y, near[n]))

    def gather_core_done(layer, batch):
        s = slot(layer, batch)
        for yy in (y, other_y):
            for n in range(depth):
                gather_core(s, other_c, yy, near[n]).wait_recv()

    def compute(layer, batch, jobs):
        s = slot(layer, batch)
        if batch == 0:
            for load in loads[layer * 2 : layer * 2 + 2]:
                load.wait()
        named = flat_rows(rows[0, :, :, :, :, pl.ds(features, LANES)]).astype(jnp.float32)
        lanes = lax.broadcasted_iota(jnp.int32, named.shape, 1)
        mine = jnp.sum(jnp.where(lanes == me + s * count, named, 0.0), axis=1, keepdims=True) > 0.5
        ups, downs = units // TILE, features // TILE
        points = ups + 2

        def run_jobs(point):
            for number, job in enumerate(jobs):
                if number * points // len(jobs) == point:
                    job()

        for j in range(ups):
            x = flat_rows(rows[s, :, :, :, :, pl.ds(0, features)])
            gate = jnp.dot(
                x, gu[layer, :, pl.ds(j * TILE, TILE)], preferred_element_type=jnp.float32
            )
            up = jnp.dot(
                x, gu[layer, :, pl.ds(units + j * TILE, TILE)], preferred_element_type=jnp.float32
            )
            value = gate / (1.0 + jnp.exp(-gate)) * up
            hidden[:, pl.ds(j * TILE, TILE)] = jnp.where(mine, value, 0.0).astype(jnp.bfloat16)
            run_jobs(j)

        def down_tile(j, carry):
            cols = pl.ds(pl.multiple_of(j * TILE, TILE), TILE)
            result = jnp.dot(hidden[...], down[layer, :, cols], preferred_element_type=jnp.float32)
            made[s, :, :, :, :, cols] = result.astype(jnp.bfloat16).reshape(
                PAIR, PAIR, depth, tokens, TILE
            )
            return carry

        lax.fori_loop(0, downs // 2, down_tile, 0)
        run_jobs(ups)
        lax.fori_loop(downs // 2, downs, down_tile, 0)
        run_jobs(ups + 1)

    def sum_core_copy(s, cc, yy):
        return remote(
            made.at[s, cc, yy], from_core.at[s, yy], rc_s.at[s, yy], rc_r.at[s, yy], core_peer
        )

    def sum_core(layer, batch):
        s = slot(layer, batch)
        go(sum_core_copy(s, other_c, other_y))
        go(sum_core_copy(s, other_c, y))

    def pair_sum(s, yy, zz):
        return made[s, c, yy, zz].astype(jnp.float32) + from_core[s, yy, zz].astype(jnp.float32)

    def sum_y_copy(s, zz):
        return remote(to_y.at[s, zz], from_y.at[s, zz], ry_s.at[s, zz], ry_r.at[s, zz], y_peer)

    def sum_y(layer, batch):
        s = slot(layer, batch)
        sum_core_copy(s, other_c, other_y).wait_recv()
        for n in reversed(range(depth)):
            zz = near[n]
            to_y[s, zz] = pair_sum(s, other_y, zz).astype(jnp.bfloat16)
            go(sum_y_copy(s, zz))
        sum_core_copy(s, other_c, y).wait_recv()

    def sum_z_step(layer, batch, n):
        s = slot(layer, batch)
        zz = near[n]
        sum_y_copy(s, zz).wait_recv()
        total = pair_sum(s, y, zz) + from_y[s, zz].astype(jnp.float32)
        to_z[s, zz] = total.astype(jnp.bfloat16)
        go(
            remote(
                to_z.at[s, zz], from_z.at[s, z], rz_s.at[s, zz], rz_r.at[s, z], expert_at(zz, y, c)
            )
        )

    def finish(layer, batch):
        s = slot(layer, batch)
        sum_y_copy(s, z).wait_recv()
        total = pair_sum(s, y, z) + from_y[s, z].astype(jnp.float32)
        for n in range(1, depth):
            zz = near[n]
            block = from_z.at[s, zz]
            remote(block, block, rz_s.at[s, zz], rz_r.at[s, zz], y_peer).wait_recv()
            total = total + from_z[s, zz].astype(jnp.float32)
        h = (x_ref[batch] if layer == 0 else out_ref[layer - 1, batch]).astype(jnp.float32)
        out_ref[layer, batch] = (h + total * 0.125).astype(jnp.bfloat16)

    def job(step, layer, batch, n=None):
        if n is None:
            return functools.partial(step, layer, batch)
        return functools.partial(step, layer, batch, n)

    def jobs_of(step, layer, batch, first):
        return [job(step, layer, batch, n) for n in range(first, depth)]

    def run(jobs):
        for one in jobs:
            one()

    def mixed(left, right):
        together = []
        for number in range(max(len(left), len(right))):
            together += left[number : number + 1] + right[number : number + 1]
        return together

    norm_send(0, 0)
    run(jobs_of(gather_z_step, 0, 0, 1))
    norm_send(0, 1)
    run(jobs_of(gather_y_step, 0, 0, 0))
    for layer in range(layers):
        gather_core_done(layer, 0)
        compute(
            layer,
            0,
            jobs_of(gather_z_step, layer, 1, 1) + jobs_of(gather_y_step, layer, 1, 0)[:2],
        )
        sum_core(layer, 0)
        sum_y(layer, 0)
        run(jobs_of(gather_y_step, layer, 1, 2))
        gather_core_done(layer, 1)
        compute(layer, 1, list(reversed(jobs_of(sum_z_step, layer, 0, 1))))
        sum_core(layer, 1)
        finish(layer, 0)
        if layer + 1 < layers:
            norm_send(layer + 1, 0)
        sum_y(layer, 1)
        later = list(reversed(jobs_of(sum_z_step, layer, 1, 1)))
        if layer + 1 < layers:
            run(mixed(later, jobs_of(gather_z_step, layer + 1, 0, 1)))
            gather_y_step(layer + 1, 0, 0)
            finish(layer, 1)
            norm_send(layer + 1, 1)
            run(jobs_of(gather_y_step, layer + 1, 0, 1))
        else:
            run(later)
            finish(layer, 1)

    for copy in sends:
        copy.wait_send()


def fused_on_device(count, inputs, routes, norm_gain, w_gate_up, w_down):
    batches, tokens, features = inputs.shape
    layers = routes.shape[0]
    units = w_down.shape[2]
    slots = layers * batches
    depth = count // (PAIR * PAIR)
    bf16 = jnp.bfloat16
    vmem = pl.BlockSpec(memory_space=pltpu.VMEM)
    hbm = pl.BlockSpec(memory_space=pl.ANY)
    dma = pltpu.SemaphoreType.DMA
    return pl.pallas_call(
        functools.partial(moe_kernel, count),
        out_shape=jax.ShapeDtypeStruct((layers, batches, tokens, features), bf16),
        in_specs=[vmem, vmem, vmem, hbm, hbm],
        out_specs=vmem,
        scratch_shapes=[
            pltpu.VMEM((layers, features, 2 * units), bf16),
            pltpu.VMEM((layers, units, features), bf16),
            pltpu.VMEM((slots, PAIR, PAIR, depth, tokens, features + LANES), bf16),
            pltpu.VMEM((count * tokens, units), bf16),
            pltpu.VMEM((slots, PAIR, PAIR, depth, tokens, features), bf16),
            pltpu.VMEM((slots, PAIR, depth, tokens, features), bf16),
            pltpu.VMEM((slots, depth, tokens, features), bf16),
            pltpu.VMEM((slots, depth, tokens, features), bf16),
            pltpu.VMEM((slots, depth, tokens, features), bf16),
            pltpu.VMEM((slots, depth, tokens, features), bf16),
            dma((layers, 2)),
            dma((slots, depth)),
            dma((slots, depth)),
            dma((slots, depth)),
            dma((slots, depth)),
            dma((slots, PAIR, depth)),
            dma((slots, PAIR, depth)),
            dma((slots, PAIR)),
            dma((slots, PAIR)),
            dma((slots, depth)),
            dma((slots, depth)),
            dma((slots, depth)),
            dma((slots, depth)),
        ],
        compiler_params=pltpu.CompilerParams(
            collective_id=0, has_side_effects=True, vmem_limit_bytes=60 << 20
        ),
        name="moe",
    )(inputs, routes, norm_gain, w_gate_up, w_down)


def choose(count, inputs, routes, norm_gain, w_gate_up, w_down):
    batches, tokens, features = inputs.shape
    layers = routes.shape[0]
    fits = layers == 2 and batches == 2 and layers * batches * count <= LANES
    tiled = w_down.shape[2] % TILE == 0 and features % (2 * TILE) == 0 and tokens % 16 == 0
    run = functools.partial(fused_on_device, count) if fits and tiled else on_device
    return run(inputs, routes, norm_gain, w_gate_up, w_down)


def solution(mesh):
    placed = (
        P(None, ("groups", "expert"), None),
        P("section", None, ("groups", "expert"), None),
        P("section", None),
        P("section", "expert", None, None),
        P("section", "expert", None, None),
    )
    count = mesh.shape["expert"]
    fused = mesh.shape["section"] == 1 and count % (PAIR * PAIR) == 0 and PAIR * PAIR < count
    return jax.shard_map(
        functools.partial(choose, count) if fused else on_device,
        mesh=mesh,
        in_specs=placed,
        out_specs=P("section", None, ("groups", "expert"), None),
        check_vma=False,
    )
```

profile of v0, /device:TPU:0, one launch (start us, length us, event | category | flops | bytes accessed | tf_op | source)
XLA Modules:
  0.0 85.0 jit_solution(17495977726524460593)
XLA Ops:
  0.0 1.4 %copy.6.routes_ref = s32[2,2,16,8]{3,2,1,0:T(8,128)} copy(s32[2,2,16,8]{2,3,1,0:T(8,128)} %param.6) | data formatting | bytes 4096 | tf_op args[1]
  1.4 82.0 %moe.1 = bf16[2,2,16,2048]{3,2,1,0:T(8,128)(2,1)} custom-call(bf16[2,16,2048]{2,1,0:T(8,128)(2,1)} %x_ref.1, s32[2,2,16,8]{3,2,1,0:T(8,128)} %copy.6.routes_ref, f32[2,2048]{1,0:T(2,128)} %gain_ref.1, bf16[2,1,2048,1536]{3,2,1,0:T(8,128)(2,1)} %gu_hbm.1, bf16[2,1,768,2048]{3,2,1,0:T(8,128)(2,1)} %down_hbm.1), custom_call_target="tpu_custom_call" | custom-call | tf_op jit(solution)/shard_map/moe/pallas_call | solution.py:422
  83.4 1.7 %copy.8 = bf16[2,2,16,2048]{3,2,1,0:T(8,128)(2,1)} copy(bf16[2,2,16,2048]{3,2,1,0:T(8,128)(2,1)} %moe.1) | data formatting | bytes 524288
where the time goes:
time: 85.3 us; the launch traced here: 85 us
  Pallas kernels  82 us (96%)
  local copies, waits for them, and re-layouts  3.08 us (4%)
    pallas_call x1, Pallas kernels, fused_on_device(): pl.pallas_call(functools.partial(moe_kernel, count), out_shape=jax.ShapeD...  82 us
    unnamed x2, local copies, waits for them, and re-layouts  3.08 us

commit v1 on v0

v1 whole, which is shorter than its diff:
```python
import functools

import jax
import jax.numpy as jnp
from jax import lax
from jax.experimental import pallas as pl
from jax.experimental.pallas import tpu as pltpu
from jax.sharding import PartitionSpec as P

eps = 1e-06


def from_behind(value, axis, steps):
    count = lax.axis_size(axis)
    initial, last = (max(0, -steps), min(count, count - steps))
    return lax.ppermute(value, axis, [(source, source + steps) for source in range(initial, last)])


def expert_rows(rows, gate_up, down_proj):
    hidden_size = down_proj.shape[0]
    joined = jnp.dot(rows, gate_up, preferred_element_type=jnp.float32)
    hidden = (jax.nn.silu(joined[:, :hidden_size]) * joined[:, hidden_size:]).astype(jnp.bfloat16)
    return jnp.dot(hidden, down_proj, preferred_element_type=jnp.float32).astype(jnp.bfloat16)


def run_experts(received, gate_up, down_proj):
    flat = received.reshape(-1, received.shape[2])
    done = expert_rows(flat, gate_up, down_proj)
    return done.reshape(received.shape)


def moe_layer(current, layer_routes, gain_row, gate_up, down_proj, experts, capacity):
    tokens, features = current.shape
    widened = current.astype(jnp.float32)
    scale_inv = lax.rsqrt(jnp.mean(widened * widened, axis=-1, keepdims=True) + eps)
    normed = (widened * scale_inv * gain_row).astype(jnp.bfloat16)
    expert_ids = jnp.arange(experts, dtype=jnp.int32)
    onehot = (layer_routes[:, :, None] == expert_ids[None, None, :]).astype(jnp.int32)
    counted = jnp.sum(onehot, axis=1)
    before = jnp.cumsum(counted, axis=0) - counted
    slot_of = jnp.sum(onehot * (expert_ids[None, None, :] * capacity + before[:, None, :]), axis=2)
    slot_ids = jnp.arange(experts * capacity, dtype=jnp.int32)
    placing = jnp.sum(
        (slot_ids[:, None, None] == slot_of[None, :, :]).astype(jnp.int32), axis=2
    ).astype(jnp.bfloat16)
    outgoing = jnp.dot(placing, normed, preferred_element_type=jnp.float32).astype(jnp.bfloat16)
    outgoing = outgoing.reshape(experts, capacity, features)
    results = run_experts(
        lax.all_to_all(outgoing, "expert", split_axis=0, concat_axis=0, tiled=True),
        gate_up,
        down_proj,
    )
    returned = lax.all_to_all(results, "expert", split_axis=0, concat_axis=0, tiled=True).reshape(
        experts * capacity, features
    )
    combined = (
        jnp.einsum("it,id->td", placing, returned, preferred_element_type=jnp.float32) * 0.125
    )
    return (widened + combined).astype(jnp.bfloat16)


def on_device(inputs, routes, norm_gain, w_gate_up, w_down):
    experts = lax.axis_size("expert")
    sections = lax.axis_size("section")
    batches, tokens, features = inputs.shape
    top_k = routes.shape[3]
    capacity = min(tokens, 2 * tokens * top_k // experts)
    if sections == 1:
        layers_out = []
        previous = [inputs[batch_no] for batch_no in range(batches)]
        for layer_no in range(routes.shape[0]):
            current_layer = []
            for batch_no in range(batches):
                current_layer.append(
                    moe_layer(
                        previous[batch_no],
                        routes[layer_no, batch_no],
                        norm_gain[layer_no],
                        w_gate_up[layer_no, 0],
                        w_down[layer_no, 0],
                        experts,
                        capacity,
                    )
                )
            layers_out.append(jnp.stack(current_layer))
            previous = current_layer
        return jnp.stack(layers_out)
    segment_no = lax.axis_index("section")
    layer_routes = routes[0]
    gain_row = norm_gain[0]
    gate_up = w_gate_up[0, 0]
    down_proj = w_down[0, 0]
    handed = jnp.zeros((tokens, features), jnp.bfloat16)
    finished = []
    for turn_no in range(batches + 1):
        if turn_no < batches:
            fresh_rows = inputs[turn_no]
        else:
            fresh_rows = jnp.zeros((tokens, features), jnp.bfloat16)
        current = jnp.where(segment_no == 0, fresh_rows, handed)
        batch_pick = jnp.clip(turn_no - segment_no, 0, batches - 1)
        turn_routes = lax.dynamic_index_in_dim(layer_routes, batch_pick, 0, keepdims=False)
        result = moe_layer(current, turn_routes, gain_row, gate_up, down_proj, experts, capacity)
        finished.append(result)
        if turn_no < batches:
            handed = from_behind(result, "section", 1)
    first_segment = jnp.stack(finished[:batches])
    second_segment = jnp.stack(finished[1:])
    return jnp.where(segment_no == 0, first_segment, second_segment)[None]

LANES = 128
PAIR = 2
DEPTH = 4
TILE = 256
CHUNKS = 2
DOWN_PARTS = 2
KINDS = ("own", "z_in", "y_in", "y_out", "z_out", "done", "up", "down")
END_ORDER = (
    0, 4, 8, 45, 33, 12, 37, 34, 77, 46, 35, 65, 38, 39, 64, 41,
    66, 69, 72, 67, 43, 192, 70, 68, 42, 71, 47, 193, 194, 73, 196, 75,
    197, 198, 224, 74, 225, 76, 78, 79, 228, 229, 200, 99, 98, 201, 202, 97,
    204, 205, 102, 103, 101, 206, 96, 232, 131, 233, 130, 236, 107, 106, 129, 237,
    105, 134, 135, 133, 108, 110, 139, 160, 111, 100, 109, 16, 138, 142, 143, 164,
    104, 20, 49, 137, 141, 168, 51, 24, 80, 53, 50, 84, 83, 54, 172, 55,
    28, 82, 57, 81, 86, 85, 61, 87, 208, 59, 209, 210, 58, 212, 89, 213,
    62, 214, 240, 91, 63, 241, 92, 244, 88, 90, 245, 94, 93, 113, 114, 216,
    95, 217, 118, 218, 117, 115, 220, 221, 119, 222, 248, 145, 249, 116, 146, 252,
    150, 253, 123, 122, 127, 126, 147, 151, 155, 121, 124, 125, 154, 159, 158, 153,
    149, 120, 157, 112, 180, 176, 188, 184,
)
INNER_ORDER = (
    0, 12, 4, 8, 33, 34, 76, 45, 35, 38, 37, 68, 39, 43, 41, 67,
    64, 66, 72, 65, 192, 47, 69, 193, 42, 194, 71, 46, 77, 70, 196, 197,
    79, 198, 73, 74, 224, 75, 78, 225, 228, 229, 200, 201, 96, 98, 101, 202,
    97, 204, 205, 102, 206, 232, 99, 233, 130, 236, 103, 237, 134, 106, 104, 107,
    131, 129, 111, 100, 109, 105, 138, 133, 135, 110, 139, 160, 164, 108, 50, 16,
    20, 51, 137, 142, 49, 53, 141, 82, 143, 54, 55, 168, 83, 24, 80, 172,
    28, 85, 84, 81, 59, 208, 87, 86, 57, 209, 61, 210, 212, 213, 62, 58,
    88, 91, 63, 214, 240, 241, 244, 245, 118, 113, 89, 93, 92, 90, 94, 95,
    216, 217, 218, 117, 119, 220, 112, 114, 221, 222, 248, 249, 115, 121, 252, 253,
    150, 122, 120, 146, 123, 116, 145, 126, 127, 125, 154, 149, 147, 151, 155, 124,
    176, 153, 158, 159, 157, 184, 180, 188,
)


def flat_rows(block):
    return block.reshape(-1, block.shape[-1])


def unpack(code):
    code, number = divmod(code, 4)
    code, chunk = divmod(code, CHUNKS)
    code, batch = divmod(code, 2)
    kind, layer = divmod(code, 2)
    return KINDS[kind], layer, batch, chunk, number


def moe_kernel(
    count,
    x_hbm,
    routes_hbm,
    gain_hbm,
    gu_hbm,
    down_hbm,
    out_ref,
    x_ref,
    routes_ref,
    gain_ref,
    gu,
    down,
    rows,
    scaled,
    squares,
    joined,
    hidden,
    made,
    from_core,
    to_y,
    from_y,
    to_z,
    from_z,
    passing,
    x_sem,
    w_sem,
    az_s,
    az_r,
    ap_s,
    ay_s,
    ay_r,
    ac_s,
    ac_r,
    rc_s,
    rc_r,
    ry_s,
    ry_r,
    rz_s,
    rz_r,
    rp_r,
):
    layers, batches = routes_ref.shape[0], routes_ref.shape[1]
    tokens, features = x_ref.shape[1], x_ref.shape[2]
    units = down.shape[1]
    width = features // CHUNKS
    me = lax.axis_index("expert")
    c = lax.rem(me, PAIR)
    y = lax.rem(lax.div(me, PAIR), PAIR)
    z = lax.div(me, PAIR * PAIR)
    other_c, other_y = 1 - c, 1 - y

    def expert_at(zz, yy, cc):
        return (zz * PAIR + yy) * PAIR + cc

    low = z < DEPTH // 2
    inner = jnp.logical_and(z > 0, z < DEPTH - 1)

    def ranked(at_end, at_inner):
        upward = jnp.where(inner, at_inner, at_end)
        return jnp.where(low, upward, DEPTH - 1 - upward)

    near = [z, ranked(1, 2), ranked(2, 0), ranked(3, 3)]
    core_peer = expert_at(z, y, other_c)
    y_peer = expert_at(z, other_y, c)
    z_peers = [me] + [expert_at(near[n], y, c) for n in range(1, DEPTH)]

    def remote(src, dst, send, recv, target):
        return pltpu.make_async_remote_copy(
            src_ref=src,
            dst_ref=dst,
            send_sem=send,
            recv_sem=recv,
            device_id={"expert": target},
            device_id_type=pl.DeviceIdType.MESH,
        )

    barrier = pltpu.get_barrier_semaphore()
    for peer in z_peers[1:] + [core_peer, y_peer]:
        pl.semaphore_signal(
            barrier, inc=1, device_id={"expert": peer}, device_id_type=pl.DeviceIdType.MESH
        )

    inputs = ((x_hbm, x_ref), (routes_hbm, routes_ref), (gain_hbm, gain_ref))
    small = [
        pltpu.make_async_copy(source, target, x_sem.at[number])
        for number, (source, target) in enumerate(inputs)
    ]
    for load in small:
        load.start()
    for load in small:
        load.wait()
    loads = []
    for layer in range(layers):
        for number, (source, target) in enumerate(((gu_hbm, gu), (down_hbm, down))):
            load = pltpu.make_async_copy(
                source.at[layer, 0], target.at[layer], w_sem.at[layer, number]
            )
            load.start()
            loads.append(load)

    lanes = lax.broadcasted_iota(jnp.int32, (LANES, tokens), 0)
    named = jnp.zeros((LANES, tokens), jnp.float32)
    for lay in range(layers):
        for bat in range(batches):
            chosen = routes_ref[lay, bat] + (lay * batches + bat) * count
            for k in range(chosen.shape[0]):
                named = named + (chosen[k : k + 1, :] == lanes).astype(jnp.float32)
    same = lax.broadcasted_iota(jnp.int32, (tokens, tokens), 0) == lax.broadcasted_iota(
        jnp.int32, (tokens, tokens), 1
    )
    named = lax.dot_general(
        same.astype(jnp.bfloat16),
        named.astype(jnp.bfloat16),
        (((1,), (1,)), ((), ())),
        preferred_element_type=jnp.float32,
    )
    rows[0, c, y, z, :, pl.ds(features, LANES)] = named.astype(jnp.bfloat16)
    for bat in range(batches):
        rows[bat, c, y, z, :, pl.ds(0, features)] = x_ref[bat]
    pl.semaphore_wait(barrier, DEPTH + 1)

    def slot(layer, batch):
        return layer * batches + batch

    def cols(h):
        return pl.ds(h * width, width)

    def row_block(s, h, cc, yy, zz):
        extra = LANES if s == 0 and h == CHUNKS - 1 else 0
        return rows.at[s, cc, yy, zz, :, pl.ds(h * width, width + extra)]

    def gather_core(s, h, cc, yy, zz):
        block = row_block(s, h, cc, yy, zz)
        return remote(block, block, ac_s.at[s, h, yy, zz], ac_r.at[s, h, yy, zz], core_peer)

    def gather_y(s, h, yy, zz):
        block = row_block(s, h, c, yy, zz)
        return remote(block, block, ay_s.at[s, h, zz], ay_r.at[s, h, zz], y_peer)

    def gather_z(s, h, n):
        block = row_block(s, h, c, y, z)
        return remote(block, block, az_s.at[s, h, n], az_r.at[s, h, z], z_peers[n])

    def gather_z_from(s, h, n):
        block = row_block(s, h, c, y, near[n])
        return remote(block, block, ap_s.at[s, h, n], az_r.at[s, h, near[n]], z_peers[2])

    def sum_core(s, h, cc, yy):
        return remote(
            made.at[s, cc, yy, :, :, cols(h)],
            from_core.at[s, yy, :, :, cols(h)],
            rc_s.at[s, h, yy],
            rc_r.at[s, h, yy],
            core_peer,
        )

    def sum_y(s, h, zz):
        return remote(
            to_y.at[s, zz, :, cols(h)],
            from_y.at[s, zz, :, cols(h)],
            ry_s.at[s, h, zz],
            ry_r.at[s, h, zz],
            y_peer,
        )

    def sum_z(s, h, n, source):
        return remote(
            to_z.at[s, near[n], :, cols(h)],
            from_z.at[s, source, :, cols(h)],
            rz_s.at[s, h, n],
            rz_r.at[s, h, source],
            z_peers[n],
        )

    def sum_pass(s, h, n):
        return remote(
            to_z.at[s, near[n], :, cols(h)],
            passing.at[s, near[n], :, cols(h)],
            rz_s.at[s, h, n],
            rp_r.at[s, h, near[n]],
            z_peers[1],
        )

    def pair_sum(s, h, yy, zz):
        return made[s, c, yy, zz, :, cols(h)].astype(jnp.float32) + from_core[
            s, yy, zz, :, cols(h)
        ].astype(jnp.float32)

    class Place:
        def __init__(self, at_end):
            self.at_end = at_end
            self.sends = []
            self.seen = set()

        def go(self, build, *args):
            build(*args).start()
            self.sends.append((build, args))

        def once(self, build, *args, key):
            if (build, key) not in self.seen:
                self.seen.add((build, key))
                build(*args).wait_recv()

        def own(self, layer, batch, h, n):
            s = slot(layer, batch)
            self.go(gather_y, s, h, y, z)
            self.go(gather_z, s, h, 1)
            self.go(gather_z, s, h, 2)
            self.go(gather_core, s, h, c, y, z)

        def z_in(self, layer, batch, h, n):
            s = slot(layer, batch)
            gather_z_from(s, h, n).wait_recv()
            if not self.at_end and n != 2:
                self.go(gather_z_from, s, h, n)
            self.go(gather_y, s, h, y, near[n])
            self.go(gather_core, s, h, c, y, near[n])

        def y_in(self, layer, batch, h, n):
            s = slot(layer, batch)
            gather_y(s, h, other_y, near[n]).wait_recv()
            self.go(gather_core, s, h, c, other_y, near[n])

        def y_out(self, layer, batch, h, n):
            s = slot(layer, batch)
            self.once(sum_core, s, h, other_c, other_y, key=(s, h, 1))
            to_y[s, near[n], :, cols(h)] = pair_sum(s, h, other_y, near[n]).astype(jnp.bfloat16)
            self.go(sum_y, s, h, near[n])

        def z_out(self, layer, batch, h, n):
            s = slot(layer, batch)
            zz = near[n]
            self.once(sum_core, s, h, other_c, y, key=(s, h, 0))
            sum_y(s, h, zz).wait_recv()
            total = pair_sum(s, h, y, zz) + from_y[s, zz, :, cols(h)].astype(jnp.float32)
            if not self.at_end and n != 2:
                sum_pass(s, h, n).wait_recv()
                total = total + passing[s, zz, :, cols(h)].astype(jnp.float32)
            to_z[s, zz, :, cols(h)] = total.astype(jnp.bfloat16)
            if self.at_end and n != 1:
                self.go(sum_pass, s, h, n)
            else:
                self.go(sum_z, s, h, n, z)

        def done(self, layer, batch, h, n):
            s = slot(layer, batch)
            self.once(sum_core, s, h, other_c, y, key=(s, h, 0))
            sum_y(s, h, z).wait_recv()
            total = pair_sum(s, h, y, z) + from_y[s, z, :, cols(h)].astype(jnp.float32)
            for r in (1, 2):
                sum_z(s, h, r, near[r]).wait_recv()
                total = total + from_z[s, near[r], :, cols(h)].astype(jnp.float32)
            source = x_ref if layer == 0 else out_ref.at[layer - 1]
            value = source[batch, :, cols(h)].astype(jnp.float32) + total * 0.125
            value = value.astype(jnp.bfloat16)
            out_ref[layer, batch, :, cols(h)] = value
            if layer + 1 < layers:
                rows[slot(layer + 1, batch), c, y, z, :, cols(h)] = value

        def drain(self):
            for build, args in self.sends:
                build(*args).wait_send()

    end, inside = Place(True), Place(False)

    def up(layer, batch, k, u):
        s = slot(layer, batch)
        if u == 0:
            for yy in (y, other_y):
                for n in range(DEPTH):
                    gather_core(s, k, other_c, yy, near[n]).wait_recv()
            if k == 0 and batch == 0:
                loads[2 * layer].wait()
            h = flat_rows(rows[s, :, :, :, :, cols(k)]).astype(jnp.float32)
            part = jnp.sum(h * h, axis=-1, keepdims=True)
            squares[...] = part if k == 0 else squares[...] + part
            scaled[...] = (h * gain_ref[pl.ds(layer, 1), cols(k)]).astype(jnp.bfloat16)
        x = scaled[...]
        mine_cols = (pl.ds(u * TILE, TILE), pl.ds(units + u * TILE, TILE))
        gate, lift = (
            jnp.dot(x, gu[layer, cols(k), where], preferred_element_type=jnp.float32)
            for where in mine_cols
        )
        if k > 0:
            gate, lift = joined[:, mine_cols[0]] + gate, joined[:, mine_cols[1]] + lift
        if k < CHUNKS - 1:
            joined[:, mine_cols[0]] = gate
            joined[:, mine_cols[1]] = lift
            return
        named = flat_rows(rows[0, :, :, :, :, pl.ds(features, LANES)]).astype(jnp.float32)
        lanes = lax.broadcasted_iota(jnp.int32, named.shape, 1)
        mine = jnp.sum(jnp.where(lanes == me + s * count, named, 0.0), axis=1, keepdims=True) > 0.5
        scale = lax.rsqrt(squares[...] * (1.0 / features) + eps)
        gate, lift = gate * scale, lift * scale
        value = gate / (1.0 + jnp.exp(-gate)) * lift
        hidden[:, pl.ds(u * TILE, TILE)] = jnp.where(mine, value, 0.0).astype(jnp.bfloat16)

    def down_part(layer, batch, h, u):
        s = slot(layer, batch)
        if h == 0 and u == 0 and batch == 0:
            loads[2 * layer + 1].wait()
        parts = DOWN_PARTS
        size = width // parts

        for j in range(size // TILE):
            where = pl.ds(h * width + u * size + j * TILE, TILE)
            result = jnp.dot(hidden[...], down[layer, :, where], preferred_element_type=jnp.float32)
            made[s, :, :, :, :, where] = result.astype(jnp.bfloat16).reshape(
                PAIR, PAIR, DEPTH, tokens, TILE
            )
        if u == parts - 1:
            for place, guard in ((end, jnp.logical_not(inner)), (inside, inner)):
                place.sends.append((sum_core, (s, h, other_c, other_y)))
                place.sends.append((sum_core, (s, h, other_c, y)))
            sum_core(s, h, other_c, other_y).start()
            sum_core(s, h, other_c, y).start()

    def steps(place, codes):
        for code in codes:
            kind, *rest = unpack(code)
            getattr(place, kind)(*rest)

    def both(codes_end, codes_inside):
        if codes_end:
            pl.when(jnp.logical_not(inner))(functools.partial(steps, end, codes_end))
        if codes_inside:
            pl.when(inner)(functools.partial(steps, inside, codes_inside))

    def split(order):
        parts, heads = [[]], []
        for code in order:
            if unpack(code)[0] in ("up", "down"):
                heads.append(code)
                parts.append([])
            else:
                parts[-1].append(code)
        return parts, heads

    parts_end, heads = split(END_ORDER)
    parts_inside, _ = split(INNER_ORDER)
    both(parts_end[0], parts_inside[0])
    for code, codes_end, codes_inside in zip(heads, parts_end[1:], parts_inside[1:]):
        kind, *rest = unpack(code)
        (up if kind == "up" else down_part)(*rest)
        both(codes_end, codes_inside)
    pl.when(jnp.logical_not(inner))(end.drain)
    pl.when(inner)(inside.drain)


def fused_on_device(count, inputs, routes, norm_gain, w_gate_up, w_down):
    batches, tokens, features = inputs.shape
    layers = routes.shape[0]
    units = w_down.shape[2]
    slots = layers * batches
    bf16 = jnp.bfloat16
    vmem = pl.BlockSpec(memory_space=pltpu.VMEM)
    hbm = pl.BlockSpec(memory_space=pl.ANY)
    dma = pltpu.SemaphoreType.DMA
    by_z = pltpu.VMEM((slots, DEPTH, tokens, features), bf16)
    every = dma((slots, CHUNKS, DEPTH))
    return pl.pallas_call(
        functools.partial(moe_kernel, count),
        out_shape=jax.ShapeDtypeStruct((layers, batches, tokens, features), bf16),
        in_specs=[hbm] * 5,
        out_specs=vmem,
        scratch_shapes=[
            pltpu.VMEM((batches, tokens, features), bf16),
            pltpu.VMEM((layers, batches, routes.shape[3], tokens), jnp.int32),
            pltpu.VMEM((layers, features), jnp.float32),
            pltpu.VMEM((layers, features, 2 * units), bf16),
            pltpu.VMEM((layers, units, features), bf16),
            pltpu.VMEM((slots, PAIR, PAIR, DEPTH, tokens, features + LANES), bf16),
            pltpu.VMEM((count * tokens, features // CHUNKS), bf16),
            pltpu.VMEM((count * tokens, 1), jnp.float32),
            pltpu.VMEM((count * tokens, 2 * units), jnp.float32),
            pltpu.VMEM((count * tokens, units), bf16),
            pltpu.VMEM((slots, PAIR, PAIR, DEPTH, tokens, features), bf16),
            pltpu.VMEM((slots, PAIR, DEPTH, tokens, features), bf16),
            by_z,
            by_z,
            by_z,
            by_z,
            by_z,
            dma((3,)),
            dma((layers, 2)),
            every,
            every,
            every,
            every,
            every,
            dma((slots, CHUNKS, PAIR, DEPTH)),
            dma((slots, CHUNKS, PAIR, DEPTH)),
            dma((slots, CHUNKS, PAIR)),
            dma((slots, CHUNKS, PAIR)),
            every,
            every,
            every,
            every,
            every,
        ],
        compiler_params=pltpu.CompilerParams(
            collective_id=0, has_side_effects=True, vmem_limit_bytes=60 << 20
        ),
        name="moe",
    )(inputs, jnp.swapaxes(routes, 2, 3), norm_gain, w_gate_up, w_down)


def choose(count, inputs, routes, norm_gain, w_gate_up, w_down):
    batches, tokens, features = inputs.shape
    layers = routes.shape[0]
    fits = layers == 2 and batches == 2 and layers * batches * count <= LANES
    tiled = w_down.shape[2] == 3 * TILE and features % (CHUNKS * DOWN_PARTS * TILE) == 0
    run = functools.partial(fused_on_device, count) if fits and tiled and tokens % 16 == 0 else on_device
    return run(inputs, routes, norm_gain, w_gate_up, w_down)


def solution(mesh):
    placed = (
        P(None, ("groups", "expert"), None),
        P("section", None, ("groups", "expert"), None),
        P("section", None),
        P("section", "expert", None, None),
        P("section", "expert", None, None),
    )
    count = mesh.shape["expert"]
    fused = mesh.shape["section"] == 1 and count == PAIR * PAIR * DEPTH
    return jax.shard_map(
        functools.partial(choose, count) if fused else on_device,
        mesh=mesh,
        in_specs=placed,
        out_specs=P("section", None, ("groups", "expert"), None),
        check_vma=False,
    )
```

time: 85.3 us -> 74.6 us (0.87)
  Pallas kernels: 82 us -> 72.8 us
  local copies, waits for them, and re-layouts: 3.08 us -> 1.67 us
    pallas_call x1, Pallas kernels: 82 us -> 72.8 us  [fused_on_device(): pl.pallas_call(functools.partial(moe_kernel, count), out_shape=jax.ShapeD...]
    unnamed x2 -> x1, local copies, waits for them, and re-layouts: 3.08 us -> 1.67 us
where the time goes in v1:
time: 74.6 us; the launch traced here: 74.5 us
  Pallas kernels  72.8 us (98%)
  local copies, waits for them, and re-layouts  1.67 us (2%)
    pallas_call x1, Pallas kernels, fused_on_device(): pl.pallas_call(functools.partial(moe_kernel, count), out_shape=jax.ShapeD...  72.8 us
    unnamed x1, local copies, waits for them, and re-layouts  1.67 us

profile of v1, /device:TPU:0, one launch (start us, length us, event | category | flops | bytes accessed | tf_op | source)
XLA Modules:
  0.0 74.5 jit_solution(9100306883125491072)
XLA Ops:
  0.0 72.8 %moe.1 = bf16[2,2,16,2048]{3,2,1,0:T(8,128)(2,1)} custom-call(bf16[2,16,2048]{2,1,0:T(8,128)(2,1)} %x_hbm.1, s32[2,2,8,16]{3,2,1,0:T(8,128)} %bitcast.1, f32[2,2048]{1,0:T(2,128)} %gain_hbm.1, bf16[2,1,2048,1536]{3,2,1,0:T(8,128)(2,1)} %gu_hbm.1, bf16[2,1,768,2048]{3,2,1,0:T(8,128)(2,1)} %down_hbm.1), custom_call_target="tpu_custom_call" | custom-call | tf_op jit(solution)/shard_map/moe/pallas_call | solution.py:519
  72.8 1.7 %copy.7 = bf16[2,2,16,2048]{3,2,1,0:T(8,128)(2,1)} copy(bf16[2,2,16,2048]{3,2,1,0:T(8,128)(2,1)} %moe.1) | data formatting | bytes 524288

commit v2 on v1

--- a/solution.py
+++ b/solution.py
@@ -116,30 +116,30 @@
 DOWN_PARTS = 2
 KINDS = ("own", "z_in", "y_in", "y_out", "z_out", "done", "up", "down")
 END_ORDER = (
-    0, 4, 8, 45, 33, 12, 37, 34, 77, 46, 35, 65, 38, 39, 64, 41,
-    66, 69, 72, 67, 43, 192, 70, 68, 42, 71, 47, 193, 194, 73, 196, 75,
-    197, 198, 224, 74, 225, 76, 78, 79, 228, 229, 200, 99, 98, 201, 202, 97,
-    204, 205, 102, 103, 101, 206, 96, 232, 131, 233, 130, 236, 107, 106, 129, 237,
-    105, 134, 135, 133, 108, 110, 139, 160, 111, 100, 109, 16, 138, 142, 143, 164,
-    104, 20, 49, 137, 141, 168, 51, 24, 80, 53, 50, 84, 83, 54, 172, 55,
-    28, 82, 57, 81, 86, 85, 61, 87, 208, 59, 209, 210, 58, 212, 89, 213,
-    62, 214, 240, 91, 63, 241, 92, 244, 88, 90, 245, 94, 93, 113, 114, 216,
-    95, 217, 118, 218, 117, 115, 220, 221, 119, 222, 248, 145, 249, 116, 146, 252,
-    150, 253, 123, 122, 127, 126, 147, 151, 155, 121, 124, 125, 154, 159, 158, 153,
-    149, 120, 157, 112, 180, 176, 188, 184,
+    0, 4, 64, 8, 12, 41, 33, 34, 37, 35, 38, 39, 45, 42, 43, 66,
+    69, 76, 67, 65, 70, 68, 192, 71, 47, 193, 73, 46, 194, 196, 197, 198,
+    224, 74, 75, 72, 225, 228, 229, 78, 98, 99, 79, 77, 96, 200, 201, 202,
+    204, 97, 101, 205, 206, 103, 232, 100, 102, 233, 130, 131, 236, 237, 129, 105,
+    107, 106, 133, 104, 108, 135, 110, 134, 137, 109, 111, 160, 16, 138, 139, 164,
+    20, 142, 143, 49, 53, 141, 81, 168, 24, 50, 51, 54, 85, 172, 28, 55,
+    84, 57, 82, 83, 61, 80, 86, 87, 208, 209, 92, 59, 210, 88, 58, 212,
+    213, 214, 93, 63, 89, 240, 241, 62, 91, 244, 114, 115, 90, 245, 216, 119,
+    118, 94, 95, 117, 217, 116, 112, 218, 220, 221, 147, 222, 248, 249, 113, 151,
+    146, 252, 121, 150, 253, 122, 123, 127, 149, 126, 145, 153, 125, 154, 155, 124,
+    180, 159, 158, 120, 157, 184, 188, 176,
 )
 INNER_ORDER = (
-    0, 12, 4, 8, 33, 34, 76, 45, 35, 38, 37, 68, 39, 43, 41, 67,
-    64, 66, 72, 65, 192, 47, 69, 193, 42, 194, 71, 46, 77, 70, 196, 197,
-    79, 198, 73, 74, 224, 75, 78, 225, 228, 229, 200, 201, 96, 98, 101, 202,
-    97, 204, 205, 102, 206, 232, 99, 233, 130, 236, 103, 237, 134, 106, 104, 107,
-    131, 129, 111, 100, 109, 105, 138, 133, 135, 110, 139, 160, 164, 108, 50, 16,
-    20, 51, 137, 142, 49, 53, 141, 82, 143, 54, 55, 168, 83, 24, 80, 172,
-    28, 85, 84, 81, 59, 208, 87, 86, 57, 209, 61, 210, 212, 213, 62, 58,
-    88, 91, 63, 214, 240, 241, 244, 245, 118, 113, 89, 93, 92, 90, 94, 95,
-    216, 217, 218, 117, 119, 220, 112, 114, 221, 222, 248, 249, 115, 121, 252, 253,
-    150, 122, 120, 146, 123, 116, 145, 126, 127, 125, 154, 149, 147, 151, 155, 124,
-    176, 153, 158, 159, 157, 184, 180, 188,
+    0, 8, 4, 12, 34, 33, 64, 41, 35, 37, 38, 39, 42, 66, 65, 43,
+    67, 192, 73, 72, 47, 46, 45, 69, 70, 68, 193, 194, 71, 196, 197, 75,
+    198, 74, 224, 225, 78, 228, 229, 77, 76, 200, 97, 103, 99, 102, 79, 201,
+    101, 96, 202, 204, 205, 98, 206, 129, 232, 233, 236, 135, 237, 131, 105, 134,
+    111, 110, 107, 106, 109, 108, 130, 104, 133, 100, 137, 143, 160, 16, 139, 138,
+    50, 164, 20, 49, 142, 51, 82, 168, 54, 141, 53, 80, 24, 81, 84, 55,
+    172, 28, 83, 58, 57, 88, 86, 85, 208, 87, 209, 59, 210, 212, 61, 213,
+    62, 90, 63, 214, 240, 241, 244, 245, 113, 91, 93, 92, 89, 94, 95, 216,
+    119, 115, 117, 217, 218, 220, 221, 222, 145, 118, 248, 249, 116, 252, 151, 147,
+    123, 253, 122, 126, 125, 149, 121, 155, 127, 120, 158, 150, 154, 124, 157, 153,
+    112, 114, 159, 146, 176, 184, 180, 188,
 )
 
 
@@ -179,7 +179,6 @@
     from_y,
     to_z,
     from_z,
-    passing,
     x_sem,
     w_sem,
     az_s,
@@ -195,7 +194,6 @@
     ry_r,
     rz_s,
     rz_r,
-    rp_r,
 ):
     layers, batches = routes_ref.shape[0], routes_ref.shape[1]
     tokens, features = x_ref.shape[1], x_ref.shape[2]
@@ -289,25 +287,25 @@
 
     def gather_core(s, h, cc, yy, zz):
         block = row_block(s, h, cc, yy, zz)
-        return remote(block, block, ac_s.at[s, h, yy, zz], ac_r.at[s, h, yy, zz], core_peer)
+        return remote(block, block, ac_s.at[s], ac_r.at[s, h, yy, zz], core_peer)
 
     def gather_y(s, h, yy, zz):
         block = row_block(s, h, c, yy, zz)
-        return remote(block, block, ay_s.at[s, h, zz], ay_r.at[s, h, zz], y_peer)
+        return remote(block, block, ay_s.at[s], ay_r.at[s, h, zz], y_peer)
 
     def gather_z(s, h, n):
         block = row_block(s, h, c, y, z)
-        return remote(block, block, az_s.at[s, h, n], az_r.at[s, h, z], z_peers[n])
+        return remote(block, block, az_s.at[s, n], az_r.at[s, h, z], z_peers[n])
 
     def gather_z_from(s, h, n):
         block = row_block(s, h, c, y, near[n])
-        return remote(block, block, ap_s.at[s, h, n], az_r.at[s, h, near[n]], z_peers[2])
+        return remote(block, block, ap_s.at[s, n], az_r.at[s, h, near[n]], z_peers[2])
 
     def sum_core(s, h, cc, yy):
         return remote(
             made.at[s, cc, yy, :, :, cols(h)],
             from_core.at[s, yy, :, :, cols(h)],
-            rc_s.at[s, h, yy],
+            rc_s.at[s],
             rc_r.at[s, h, yy],
             core_peer,
         )
@@ -316,7 +314,7 @@
         return remote(
             to_y.at[s, zz, :, cols(h)],
             from_y.at[s, zz, :, cols(h)],
-            ry_s.at[s, h, zz],
+            ry_s.at[s],
             ry_r.at[s, h, zz],
             y_peer,
         )
@@ -325,18 +323,9 @@
         return remote(
             to_z.at[s, near[n], :, cols(h)],
             from_z.at[s, source, :, cols(h)],
-            rz_s.at[s, h, n],
+            rz_s.at[s],
             rz_r.at[s, h, source],
             z_peers[n],
-        )
-
-    def sum_pass(s, h, n):
-        return remote(
-            to_z.at[s, near[n], :, cols(h)],
-            passing.at[s, near[n], :, cols(h)],
-            rz_s.at[s, h, n],
-            rp_r.at[s, h, near[n]],
-            z_peers[1],
         )
 
     def pair_sum(s, h, yy, zz):
@@ -347,12 +336,7 @@
     class Place:
         def __init__(self, at_end):
             self.at_end = at_end
-            self.sends = []
             self.seen = set()
-
-        def go(self, build, *args):
-            build(*args).start()
-            self.sends.append((build, args))
 
         def once(self, build, *args, key):
             if (build, key) not in self.seen:
@@ -361,29 +345,29 @@
 
         def own(self, layer, batch, h, n):
             s = slot(layer, batch)
-            self.go(gather_y, s, h, y, z)
-            self.go(gather_z, s, h, 1)
-            self.go(gather_z, s, h, 2)
-            self.go(gather_core, s, h, c, y, z)
+            gather_y(s, h, y, z).start()
+            gather_z(s, h, 1).start()
+            gather_z(s, h, 2).start()
+            gather_core(s, h, c, y, z).start()
 
         def z_in(self, layer, batch, h, n):
             s = slot(layer, batch)
             gather_z_from(s, h, n).wait_recv()
             if not self.at_end and n != 2:
-                self.go(gather_z_from, s, h, n)
-            self.go(gather_y, s, h, y, near[n])
-            self.go(gather_core, s, h, c, y, near[n])
+                gather_z_from(s, h, n).start()
+            gather_y(s, h, y, near[n]).start()
+            gather_core(s, h, c, y, near[n]).start()
 
         def y_in(self, layer, batch, h, n):
             s = slot(layer, batch)
             gather_y(s, h, other_y, near[n]).wait_recv()
-            self.go(gather_core, s, h, c, other_y, near[n])
+            gather_core(s, h, c, other_y, near[n]).start()
 
         def y_out(self, layer, batch, h, n):
             s = slot(layer, batch)
             self.once(sum_core, s, h, other_c, other_y, key=(s, h, 1))
             to_y[s, near[n], :, cols(h)] = pair_sum(s, h, other_y, near[n]).astype(jnp.bfloat16)
-            self.go(sum_y, s, h, near[n])
+            sum_y(s, h, near[n]).start()
 
         def z_out(self, layer, batch, h, n):
             s = slot(layer, batch)
@@ -391,21 +375,15 @@
             self.once(sum_core, s, h, other_c, y, key=(s, h, 0))
             sum_y(s, h, zz).wait_recv()
             total = pair_sum(s, h, y, zz) + from_y[s, zz, :, cols(h)].astype(jnp.float32)
-            if not self.at_end and n != 2:
-                sum_pass(s, h, n).wait_recv()
-                total = total + passing[s, zz, :, cols(h)].astype(jnp.float32)
             to_z[s, zz, :, cols(h)] = total.astype(jnp.bfloat16)
-            if self.at_end and n != 1:
-                self.go(sum_pass, s, h, n)
-            else:
-                self.go(sum_z, s, h, n, z)
+            sum_z(s, h, n, z).start()
 
         def done(self, layer, batch, h, n):
             s = slot(layer, batch)
             self.once(sum_core, s, h, other_c, y, key=(s, h, 0))
             sum_y(s, h, z).wait_recv()
             total = pair_sum(s, h, y, z) + from_y[s, z, :, cols(h)].astype(jnp.float32)
-            for r in (1, 2):
+            for r in range(1, DEPTH):
                 sum_z(s, h, r, near[r]).wait_recv()
                 total = total + from_z[s, near[r], :, cols(h)].astype(jnp.float32)
             source = x_ref if layer == 0 else out_ref.at[layer - 1]
@@ -414,10 +392,6 @@
             out_ref[layer, batch, :, cols(h)] = value
             if layer + 1 < layers:
                 rows[slot(layer + 1, batch), c, y, z, :, cols(h)] = value
-
-        def drain(self):
-            for build, args in self.sends:
-                build(*args).wait_send()
 
     end, inside = Place(True), Place(False)
 
@@ -467,9 +441,6 @@
                 PAIR, PAIR, DEPTH, tokens, TILE
             )
         if u == parts - 1:
-            for place, guard in ((end, jnp.logical_not(inner)), (inside, inner)):
-                place.sends.append((sum_core, (s, h, other_c, other_y)))
-                place.sends.append((sum_core, (s, h, other_c, y)))
             sum_core(s, h, other_c, other_y).start()
             sum_core(s, h, other_c, y).start()
 
@@ -501,8 +472,25 @@
         kind, *rest = unpack(code)
         (up if kind == "up" else down_part)(*rest)
         both(codes_end, codes_inside)
-    pl.when(jnp.logical_not(inner))(end.drain)
-    pl.when(inner)(inside.drain)
+    def sent(block, sem):
+        remote(block, block, sem, sem, core_peer).wait_send()
+
+    for s in range(layers * batches):
+        wide = pl.ds(0, features + (LANES if s == 0 else 0))
+        sent(rows.at[s, c, :, :, :, wide], ac_s.at[s])
+        sent(rows.at[s, c, y, :, :, wide], ay_s.at[s])
+        sent(rows.at[s, c, y, z, :, wide], az_s.at[s, 1])
+        sent(rows.at[s, c, y, z, :, wide], az_s.at[s, 2])
+        sent(made.at[s, other_c], rc_s.at[s])
+        sent(to_y.at[s], ry_s.at[s])
+        sent(to_z.at[s, pl.ds(0, DEPTH - 1)], rz_s.at[s])
+
+    @pl.when(inner)
+    def _():
+        for s in range(layers * batches):
+            wide = pl.ds(0, features + (LANES if s == 0 else 0))
+            sent(rows.at[s, c, y, z, :, wide], ap_s.at[s, 1])
+            sent(rows.at[s, c, y, z, :, wide], ap_s.at[s, 3])
 
 
 def fused_on_device(count, inputs, routes, norm_gain, w_gate_up, w_down):
@@ -518,7 +506,7 @@
     every = dma((slots, CHUNKS, DEPTH))
     return pl.pallas_call(
         functools.partial(moe_kernel, count),
-        out_shape=jax.ShapeDtypeStruct((layers, batches, tokens, features), bf16),
+        out_shape=pltpu.VMEM((layers, batches, tokens, features), bf16),
         in_specs=[hbm] * 5,
         out_specs=vmem,
         scratch_shapes=[
@@ -538,26 +526,24 @@
             by_z,
             by_z,
             by_z,
-            by_z,
             dma((3,)),
             dma((layers, 2)),
+            dma((slots, DEPTH)),
             every,
+            dma((slots, DEPTH)),
+            dma((slots,)),
             every,
+            dma((slots,)),
+            dma((slots, CHUNKS, PAIR, DEPTH)),
+            dma((slots,)),
+            dma((slots, CHUNKS, PAIR)),
+            dma((slots,)),
             every,
-            every,
-            every,
-            dma((slots, CHUNKS, PAIR, DEPTH)),
-            dma((slots, CHUNKS, PAIR, DEPTH)),
-            dma((slots, CHUNKS, PAIR)),
-            dma((slots, CHUNKS, PAIR)),
-            every,
-            every,
-            every,
-            every,
+            dma((slots,)),
             every,
         ],
         compiler_params=pltpu.CompilerParams(
-            collective_id=0, has_side_effects=True, vmem_limit_bytes=60 << 20
+            collective_id=0, has_side_effects=True, vmem_limit_bytes=58 << 20
         ),
         name="moe",
     )(inputs, jnp.swapaxes(routes, 2, 3), norm_gain, w_gate_up, w_down)

time: 74.6 us -> 70.2 us (0.941)
  Pallas kernels: 72.8 us -> 69.3 us
  local copies, waits for them, and re-layouts: 1.67 us -> 0.71 us
    pallas_call x1, Pallas kernels: 72.8 us -> 69.3 us  [fused_on_device(): pl.pallas_call(functools.partial(moe_kernel, count), out_shape=pltpu.VMEM...]
    unnamed x1, local copies, waits for them, and re-layouts: 1.67 us -> 0.71 us
where the time goes in v2:
time: 70.2 us; the launch traced here: 70.1 us
  Pallas kernels  69.3 us (99%)
  local copies, waits for them, and re-layouts  0.71 us (1%)
    pallas_call x1, Pallas kernels, fused_on_device(): pl.pallas_call(functools.partial(moe_kernel, count), out_shape=pltpu.VMEM...  69.3 us

profile of v2, /device:TPU:0, one launch (start us, length us, event | category | flops | bytes accessed | tf_op | source)
XLA Modules:
  0.0 70.1 jit_solution(8489661560083562417)
XLA Ops:
  0.0 69.3 %moe.1 = bf16[2,2,16,2048]{3,2,1,0:T(8,128)(2,1)S(1)} custom-call(bf16[2,16,2048]{2,1,0:T(8,128)(2,1)} %x_hbm.1, s32[2,2,8,16]{3,2,1,0:T(8,128)} %bitcast.1, f32[2,2048]{1,0:T(2,128)} %gain_hbm.1, bf16[2,1,2048,1536]{3,2,1,0:T(8,128)(2,1)} %gu_hbm.1, bf16[2,1,768,2048]{3,2,1,0:T(8,128)(2,1)} %down_hbm.1), custom_call_target="tpu_custom_call" | custom-call | tf_op jit(solution)/shard_map/moe/pallas_call | solution.py:507
  69.4 0.7 %copy.7 = bf16[2,2,16,2048]{3,2,1,0:T(8,128)(2,1)} copy(bf16[2,2,16,2048]{3,2,1,0:T(8,128)(2,1)S(1)} %moe.1) | data formatting | bytes 524288

commit v3 on v2

--- a/solution.py
+++ b/solution.py
@@ -113,33 +113,69 @@
 DEPTH = 4
 TILE = 256
 CHUNKS = 2
-DOWN_PARTS = 2
+DOWN_PARTS = 1
 KINDS = ("own", "z_in", "y_in", "y_out", "z_out", "done", "up", "down")
-END_ORDER = (
-    0, 4, 64, 8, 12, 41, 33, 34, 37, 35, 38, 39, 45, 42, 43, 66,
-    69, 76, 67, 65, 70, 68, 192, 71, 47, 193, 73, 46, 194, 196, 197, 198,
-    224, 74, 75, 72, 225, 228, 229, 78, 98, 99, 79, 77, 96, 200, 201, 202,
-    204, 97, 101, 205, 206, 103, 232, 100, 102, 233, 130, 131, 236, 237, 129, 105,
-    107, 106, 133, 104, 108, 135, 110, 134, 137, 109, 111, 160, 16, 138, 139, 164,
-    20, 142, 143, 49, 53, 141, 81, 168, 24, 50, 51, 54, 85, 172, 28, 55,
-    84, 57, 82, 83, 61, 80, 86, 87, 208, 209, 92, 59, 210, 88, 58, 212,
-    213, 214, 93, 63, 89, 240, 241, 62, 91, 244, 114, 115, 90, 245, 216, 119,
-    118, 94, 95, 117, 217, 116, 112, 218, 220, 221, 147, 222, 248, 249, 113, 151,
-    146, 252, 121, 150, 253, 122, 123, 127, 149, 126, 145, 153, 125, 154, 155, 124,
-    180, 159, 158, 120, 157, 184, 188, 176,
-)
-INNER_ORDER = (
-    0, 8, 4, 12, 34, 33, 64, 41, 35, 37, 38, 39, 42, 66, 65, 43,
-    67, 192, 73, 72, 47, 46, 45, 69, 70, 68, 193, 194, 71, 196, 197, 75,
-    198, 74, 224, 225, 78, 228, 229, 77, 76, 200, 97, 103, 99, 102, 79, 201,
-    101, 96, 202, 204, 205, 98, 206, 129, 232, 233, 236, 135, 237, 131, 105, 134,
-    111, 110, 107, 106, 109, 108, 130, 104, 133, 100, 137, 143, 160, 16, 139, 138,
-    50, 164, 20, 49, 142, 51, 82, 168, 54, 141, 53, 80, 24, 81, 84, 55,
-    172, 28, 83, 58, 57, 88, 86, 85, 208, 87, 209, 59, 210, 212, 61, 213,
-    62, 90, 63, 214, 240, 241, 244, 245, 113, 91, 93, 92, 89, 94, 95, 216,
-    119, 115, 117, 217, 218, 220, 221, 222, 145, 118, 248, 249, 116, 252, 151, 147,
-    123, 253, 122, 126, 125, 149, 121, 155, 127, 120, 158, 150, 154, 124, 157, 153,
-    112, 114, 159, 146, 176, 184, 180, 188,
+ORDERS = (
+    (
+        (
+            0, 8, 24, 16, 81, 128, 65, 136, 73, 152, 89, 144, 82, 129, 66, 67,
+            153, 137, 74, 146, 90, 130, 75, 131, 384, 145, 385, 386, 91, 138, 154, 83,
+            139, 392, 393, 394, 448, 155, 456, 388, 389, 147, 390, 396, 397, 195, 193, 194,
+            398, 201, 203, 202, 200, 452, 460, 400, 401, 402, 408, 409, 410, 259, 192, 464,
+            257, 472, 258, 404, 267, 405, 406, 266, 412, 413, 208, 209, 210, 211, 414, 216,
+            265, 219, 218, 217, 468, 476, 320, 32, 273, 274, 328, 40, 275, 283, 97, 282,
+            281, 160, 105, 168, 161, 98, 99, 169, 106, 336, 162, 48, 113, 344, 56, 107,
+            163, 416, 417, 418, 170, 176, 114, 177, 184, 121, 171, 424, 425, 426, 480, 488,
+            178, 420, 115, 421, 422, 122, 185, 123, 224, 226, 225, 227, 234, 235, 232, 233,
+            428, 429, 430, 179, 484, 186, 492, 187, 432, 433, 434, 290, 440, 441, 289, 291,
+            442, 496, 298, 504, 299, 241, 242, 240, 243, 297, 436, 437, 249, 250, 251, 248,
+            438, 444, 445, 446, 500, 352, 508, 305, 306, 307, 313, 360, 314, 315, 368, 376,
+        ),
+        (
+            8, 24, 0, 16, 89, 73, 65, 128, 144, 81, 90, 153, 152, 137, 136, 74,
+            145, 75, 66, 154, 82, 91, 129, 138, 139, 67, 384, 130, 385, 386, 146, 83,
+            155, 392, 131, 393, 394, 448, 456, 147, 388, 389, 390, 396, 397, 398, 452, 460,
+            400, 401, 194, 193, 195, 402, 408, 201, 203, 192, 409, 410, 464, 472, 404, 405,
+            406, 412, 413, 258, 414, 257, 468, 476, 259, 200, 202, 265, 208, 210, 209, 211,
+            267, 219, 217, 266, 216, 320, 32, 274, 273, 97, 218, 328, 40, 275, 283, 281,
+            282, 160, 161, 168, 98, 105, 416, 99, 417, 336, 162, 48, 418, 344, 56, 113,
+            106, 169, 107, 424, 163, 176, 425, 114, 426, 121, 480, 488, 177, 420, 170, 421,
+            422, 171, 428, 429, 430, 484, 178, 185, 122, 492, 184, 115, 123, 432, 433, 434,
+            225, 226, 224, 227, 234, 235, 232, 233, 440, 441, 442, 496, 179, 504, 436, 437,
+            438, 187, 186, 444, 289, 445, 290, 446, 500, 291, 299, 508, 298, 297, 241, 242,
+            243, 240, 251, 250, 249, 248, 305, 306, 360, 352, 307, 315, 314, 313, 368, 376,
+        ),
+    ),
+    (
+        (
+            16, 0, 8, 24, 66, 81, 144, 65, 136, 67, 74, 152, 73, 130, 128, 89,
+            75, 129, 131, 384, 90, 385, 91, 82, 386, 138, 137, 83, 153, 139, 392, 145,
+            393, 394, 448, 155, 154, 456, 146, 388, 389, 390, 396, 193, 195, 194, 192, 397,
+            202, 203, 147, 200, 398, 201, 452, 460, 400, 401, 402, 408, 409, 257, 410, 464,
+            259, 472, 258, 404, 266, 405, 406, 267, 412, 210, 208, 211, 209, 413, 216, 265,
+            219, 218, 414, 468, 476, 217, 274, 275, 273, 320, 32, 283, 282, 328, 40, 281,
+            97, 98, 160, 168, 99, 105, 161, 106, 336, 48, 162, 107, 163, 416, 417, 169,
+            170, 418, 176, 113, 344, 56, 171, 424, 425, 426, 480, 114, 488, 420, 177, 421,
+            122, 422, 115, 121, 184, 123, 224, 227, 225, 226, 232, 233, 234, 428, 178, 429,
+            430, 186, 484, 179, 185, 492, 235, 432, 187, 433, 434, 440, 441, 291, 442, 289,
+            496, 504, 290, 297, 242, 240, 243, 241, 298, 248, 250, 249, 251, 436, 437, 299,
+            438, 444, 445, 446, 500, 508, 306, 352, 307, 305, 314, 313, 315, 360, 368, 376,
+        ),
+        (
+            24, 8, 0, 16, 89, 152, 74, 136, 128, 73, 144, 75, 90, 65, 153, 81,
+            138, 91, 66, 137, 67, 139, 82, 384, 385, 386, 154, 83, 129, 145, 130, 392,
+            393, 131, 394, 448, 146, 456, 147, 388, 389, 390, 396, 397, 398, 452, 460, 400,
+            401, 402, 408, 193, 194, 192, 195, 409, 201, 200, 155, 202, 203, 410, 464, 472,
+            404, 405, 406, 412, 413, 414, 257, 468, 258, 476, 259, 265, 209, 210, 208, 211,
+            266, 218, 219, 217, 267, 273, 216, 274, 320, 32, 275, 283, 282, 281, 160, 97,
+            328, 40, 98, 416, 99, 417, 418, 161, 336, 48, 106, 105, 162, 107, 163, 168,
+            424, 425, 113, 426, 344, 56, 176, 480, 170, 488, 169, 420, 171, 421, 422, 428,
+            429, 114, 430, 177, 484, 121, 122, 492, 115, 123, 225, 226, 227, 432, 433, 233,
+            178, 234, 184, 224, 232, 235, 434, 440, 441, 442, 496, 504, 185, 186, 179, 436,
+            437, 438, 187, 444, 445, 446, 500, 289, 291, 290, 508, 297, 298, 243, 242, 299,
+            240, 241, 250, 251, 249, 248, 307, 306, 352, 305, 314, 315, 313, 368, 376, 360,
+        ),
+    ),
 )
 
 
@@ -148,7 +184,7 @@
 
 
 def unpack(code):
-    code, number = divmod(code, 4)
+    code, number = divmod(code, 8)
     code, chunk = divmod(code, CHUNKS)
     code, batch = divmod(code, 2)
     kind, layer = divmod(code, 2)
@@ -278,16 +314,15 @@
     def slot(layer, batch):
         return layer * batches + batch
 
-    def cols(h):
-        return pl.ds(h * width, width)
+    def cols(h, s=None):
+        return pl.ds(h * width, width + (LANES if s == 0 and h == CHUNKS - 1 else 0))
 
     def row_block(s, h, cc, yy, zz):
-        extra = LANES if s == 0 and h == CHUNKS - 1 else 0
-        return rows.at[s, cc, yy, zz, :, pl.ds(h * width, width + extra)]
+        return rows.at[s, cc, yy, zz, :, cols(h, s)]
 
     def gather_core(s, h, cc, yy, zz):
         block = row_block(s, h, cc, yy, zz)
-        return remote(block, block, ac_s.at[s], ac_r.at[s, h, yy, zz], core_peer)
+        return remote(block, block, ac_s.at[s], ac_r.at[s, h], core_peer)
 
     def gather_y(s, h, yy, zz):
         block = row_block(s, h, c, yy, zz)
@@ -334,8 +369,10 @@
         ].astype(jnp.float32)
 
     class Place:
-        def __init__(self, at_end):
-            self.at_end = at_end
+        def __init__(self, is_inner, core):
+            self.at_end = not is_inner
+            self.here = jnp.logical_and(inner if is_inner else jnp.logical_not(inner), c == core)
+            self.steps = ORDERS[is_inner][core]
             self.seen = set()
 
         def once(self, build, *args, key):
@@ -393,17 +430,26 @@
             if layer + 1 < layers:
                 rows[slot(layer + 1, batch), c, y, z, :, cols(h)] = value
 
-    end, inside = Place(True), Place(False)
-
-    def up(layer, batch, k, u):
+    places = [Place(is_inner, core) for is_inner in (0, 1) for core in range(PAIR)]
+    loaded = set()
+
+    def weights(number):
+        if number not in loaded:
+            loaded.add(number)
+            loads[number].wait()
+
+    def up(layer, batch, k, number):
         s = slot(layer, batch)
+        cc, u = divmod(number, 4)
         if u == 0:
-            for yy in (y, other_y):
-                for n in range(DEPTH):
-                    gather_core(s, k, other_c, yy, near[n]).wait_recv()
-            if k == 0 and batch == 0:
-                loads[2 * layer].wait()
-            h = flat_rows(rows[s, :, :, :, :, cols(k)]).astype(jnp.float32)
+
+            @pl.when(c != cc)
+            def _():
+                block = rows.at[s, other_c, :, :, :, cols(k, s)]
+                remote(block, block, ac_s.at[s], ac_r.at[s, k], core_peer).wait_recv()
+
+            weights(2 * layer)
+            h = flat_rows(rows[s, cc, :, :, :, cols(k)]).astype(jnp.float32)
             part = jnp.sum(h * h, axis=-1, keepdims=True)
             squares[...] = part if k == 0 else squares[...] + part
             scaled[...] = (h * gain_ref[pl.ds(layer, 1), cols(k)]).astype(jnp.bfloat16)
@@ -419,7 +465,7 @@
             joined[:, mine_cols[0]] = gate
             joined[:, mine_cols[1]] = lift
             return
-        named = flat_rows(rows[0, :, :, :, :, pl.ds(features, LANES)]).astype(jnp.float32)
+        named = flat_rows(rows[0, cc, :, :, :, pl.ds(features, LANES)]).astype(jnp.float32)
         lanes = lax.broadcasted_iota(jnp.int32, named.shape, 1)
         mine = jnp.sum(jnp.where(lanes == me + s * count, named, 0.0), axis=1, keepdims=True) > 0.5
         scale = lax.rsqrt(squares[...] * (1.0 / features) + eps)
@@ -427,33 +473,28 @@
         value = gate / (1.0 + jnp.exp(-gate)) * lift
         hidden[:, pl.ds(u * TILE, TILE)] = jnp.where(mine, value, 0.0).astype(jnp.bfloat16)
 
-    def down_part(layer, batch, h, u):
+    def down_part(layer, batch, h, number):
         s = slot(layer, batch)
-        if h == 0 and u == 0 and batch == 0:
-            loads[2 * layer + 1].wait()
-        parts = DOWN_PARTS
-        size = width // parts
-
+        cc, u = divmod(number, 4)
+        weights(2 * layer + 1)
+        size = width // DOWN_PARTS
         for j in range(size // TILE):
             where = pl.ds(h * width + u * size + j * TILE, TILE)
             result = jnp.dot(hidden[...], down[layer, :, where], preferred_element_type=jnp.float32)
-            made[s, :, :, :, :, where] = result.astype(jnp.bfloat16).reshape(
-                PAIR, PAIR, DEPTH, tokens, TILE
+            made[s, cc, :, :, :, where] = result.astype(jnp.bfloat16).reshape(
+                PAIR, DEPTH, tokens, TILE
             )
-        if u == parts - 1:
-            sum_core(s, h, other_c, other_y).start()
-            sum_core(s, h, other_c, y).start()
+        if u == DOWN_PARTS - 1:
+
+            @pl.when(c != cc)
+            def _():
+                sum_core(s, h, other_c, other_y).start()
+                sum_core(s, h, other_c, y).start()
 
     def steps(place, codes):
         for code in codes:
             kind, *rest = unpack(code)
             getattr(place, kind)(*rest)
-
-    def both(codes_end, codes_inside):
-        if codes_end:
-            pl.when(jnp.logical_not(inner))(functools.partial(steps, end, codes_end))
-        if codes_inside:
-            pl.when(inner)(functools.partial(steps, inside, codes_inside))
 
     def split(order):
         parts, heads = [[]], []
@@ -465,13 +506,15 @@
                 parts[-1].append(code)
         return parts, heads
 
-    parts_end, heads = split(END_ORDER)
-    parts_inside, _ = split(INNER_ORDER)
-    both(parts_end[0], parts_inside[0])
-    for code, codes_end, codes_inside in zip(heads, parts_end[1:], parts_inside[1:]):
-        kind, *rest = unpack(code)
-        (up if kind == "up" else down_part)(*rest)
-        both(codes_end, codes_inside)
+    pieces = [split(place.steps) for place in places]
+    for number, code in enumerate([None] + pieces[0][1]):
+        if code is not None:
+            kind, *rest = unpack(code)
+            (up if kind == "up" else down_part)(*rest)
+        for place, (parts, heads) in zip(places, pieces):
+            if parts[number]:
+                pl.when(place.here)(functools.partial(steps, place, parts[number]))
+
     def sent(block, sem):
         remote(block, block, sem, sem, core_peer).wait_send()
 
@@ -498,6 +541,7 @@
     layers = routes.shape[0]
     units = w_down.shape[2]
     slots = layers * batches
+    half = count * tokens // PAIR
     bf16 = jnp.bfloat16
     vmem = pl.BlockSpec(memory_space=pltpu.VMEM)
     hbm = pl.BlockSpec(memory_space=pl.ANY)
@@ -516,10 +560,10 @@
             pltpu.VMEM((layers, features, 2 * units), bf16),
             pltpu.VMEM((layers, units, features), bf16),
             pltpu.VMEM((slots, PAIR, PAIR, DEPTH, tokens, features + LANES), bf16),
-            pltpu.VMEM((count * tokens, features // CHUNKS), bf16),
-            pltpu.VMEM((count * tokens, 1), jnp.float32),
-            pltpu.VMEM((count * tokens, 2 * units), jnp.float32),
-            pltpu.VMEM((count * tokens, units), bf16),
+            pltpu.VMEM((half, features // CHUNKS), bf16),
+            pltpu.VMEM((half, 1), jnp.float32),
+            pltpu.VMEM((half, 2 * units), jnp.float32),
+            pltpu.VMEM((half, units), bf16),
             pltpu.VMEM((slots, PAIR, PAIR, DEPTH, tokens, features), bf16),
             pltpu.VMEM((slots, PAIR, DEPTH, tokens, features), bf16),
             by_z,
@@ -534,7 +578,7 @@
             dma((slots,)),
             every,
             dma((slots,)),
-            dma((slots, CHUNKS, PAIR, DEPTH)),
+            dma((slots, CHUNKS)),
             dma((slots,)),
             dma((slots, CHUNKS, PAIR)),
             dma((slots,)),

time: 70.2 us -> 69.3 us (0.987)
  the two profiles are of different devices: /device:TPU:0 before, /device:TPU:1 now
where the time goes in v3:
time: 69.3 us; the launch traced here: 69.2 us
  Pallas kernels  68.4 us (99%)
  local copies, waits for them, and re-layouts  0.71 us (1%)
    pallas_call x1, Pallas kernels, fused_on_device(): pl.pallas_call(functools.partial(moe_kernel, count), out_shape=pltpu.VMEM...  68.4 us

profile of v3, /device:TPU:1, one launch (start us, length us, event | category | flops | bytes accessed | tf_op | source)
XLA Modules:
  0.0 69.2 jit_solution(8471691553855085038)
XLA Ops:
  0.0 68.4 %moe.1 = bf16[2,2,16,2048]{3,2,1,0:T(8,128)(2,1)S(1)} custom-call(bf16[2,16,2048]{2,1,0:T(8,128)(2,1)} %x_hbm.1, s32[2,2,8,16]{3,2,1,0:T(8,128)} %bitcast.1, f32[2,2048]{1,0:T(2,128)} %gain_hbm.1, bf16[2,1,2048,1536]{3,2,1,0:T(8,128)(2,1)} %gu_hbm.1, bf16[2,1,768,2048]{3,2,1,0:T(8,128)(2,1)} %down_hbm.1), custom_call_target="tpu_custom_call" | custom-call | tf_op jit(solution)/shard_map/moe/pallas_call | solution.py:551
  68.5 0.7 %copy.7 = bf16[2,2,16,2048]{3,2,1,0:T(8,128)(2,1)} copy(bf16[2,2,16,2048]{3,2,1,0:T(8,128)(2,1)S(1)} %moe.1) | data formatting | bytes 524288

commit v4 on v3

--- a/solution.py
+++ b/solution.py
@@ -326,22 +326,22 @@
 
     def gather_y(s, h, yy, zz):
         block = row_block(s, h, c, yy, zz)
-        return remote(block, block, ay_s.at[s], ay_r.at[s, h, zz], y_peer)
+        return remote(block, block, ay_s.at[s], ay_r.at[s % PAIR, h, zz], y_peer)
 
     def gather_z(s, h, n):
         block = row_block(s, h, c, y, z)
-        return remote(block, block, az_s.at[s, n], az_r.at[s, h, z], z_peers[n])
+        return remote(block, block, az_s.at[s, n], az_r.at[s % PAIR, h, z], z_peers[n])
 
     def gather_z_from(s, h, n):
         block = row_block(s, h, c, y, near[n])
-        return remote(block, block, ap_s.at[s, n], az_r.at[s, h, near[n]], z_peers[2])
+        return remote(block, block, ap_s.at[s, n], az_r.at[s % PAIR, h, near[n]], z_peers[2])
 
     def sum_core(s, h, cc, yy):
         return remote(
             made.at[s, cc, yy, :, :, cols(h)],
             from_core.at[s, yy, :, :, cols(h)],
             rc_s.at[s],
-            rc_r.at[s, h, yy],
+            rc_r.at[s % PAIR, h, yy],
             core_peer,
         )
 
@@ -350,7 +350,7 @@
             to_y.at[s, zz, :, cols(h)],
             from_y.at[s, zz, :, cols(h)],
             ry_s.at[s],
-            ry_r.at[s, h, zz],
+            ry_r.at[s % PAIR, h, zz],
             y_peer,
         )
 
@@ -359,7 +359,7 @@
             to_z.at[s, near[n], :, cols(h)],
             from_z.at[s, source, :, cols(h)],
             rz_s.at[s],
-            rz_r.at[s, h, source],
+            rz_r.at[s % PAIR, h, source],
             z_peers[n],
         )
 
@@ -547,7 +547,7 @@
     hbm = pl.BlockSpec(memory_space=pl.ANY)
     dma = pltpu.SemaphoreType.DMA
     by_z = pltpu.VMEM((slots, DEPTH, tokens, features), bf16)
-    every = dma((slots, CHUNKS, DEPTH))
+    every = dma((batches, CHUNKS, DEPTH))
     return pl.pallas_call(
         functools.partial(moe_kernel, count),
         out_shape=pltpu.VMEM((layers, batches, tokens, features), bf16),
@@ -580,7 +580,7 @@
             dma((slots,)),
             dma((slots, CHUNKS)),
             dma((slots,)),
-            dma((slots, CHUNKS, PAIR)),
+            dma((batches, CHUNKS, PAIR)),
             dma((slots,)),
             every,
             dma((slots,)),

time: 69.3 us -> 68.7 us (level)
  the two profiles are of different devices: /device:TPU:1 before, /device:TPU:0 now
where the time goes in v4:
time: 68.7 us; the launch traced here: 67.4 us
  Pallas kernels  66.7 us (97%)
  local copies, waits for them, and re-layouts  0.71 us (1%)
    pallas_call x1, Pallas kernels, fused_on_device(): pl.pallas_call(functools.partial(moe_kernel, count), out_shape=pltpu.VMEM...  66.7 us

profile of v4, /device:TPU:0, one launch (start us, length us, event | category | flops | bytes accessed | tf_op | source)
XLA Modules:
  0.0 67.4 jit_solution(3487348900231557662)
XLA Ops:
  0.0 66.7 %moe.1 = bf16[2,2,16,2048]{3,2,1,0:T(8,128)(2,1)S(1)} custom-call(bf16[2,16,2048]{2,1,0:T(8,128)(2,1)} %x_hbm.1, s32[2,2,8,16]{3,2,1,0:T(8,128)} %bitcast.1, f32[2,2048]{1,0:T(2,128)} %gain_hbm.1, bf16[2,1,2048,1536]{3,2,1,0:T(8,128)(2,1)} %gu_hbm.1, bf16[2,1,768,2048]{3,2,1,0:T(8,128)(2,1)} %down_hbm.1), custom_call_target="tpu_custom_call" | custom-call | tf_op jit(solution)/shard_map/moe/pallas_call | solution.py:551
  66.7 0.7 %copy.7 = bf16[2,2,16,2048]{3,2,1,0:T(8,128)(2,1)} copy(bf16[2,2,16,2048]{3,2,1,0:T(8,128)(2,1)S(1)} %moe.1) | data formatting | bytes 524288
